TPU v7x, 512 devices: a whole 4x8x8 slice. The times are simulated.
512 devices in a mesh: tm: 16 (over z_lo, x, core), height: 32 (over y, z_hi).
Axes of the slice: x: 4, y: 8, z: 8 (z_hi: 4, z_lo: 2; z = z_hi * 2 + z_lo), core: 2. Of those that a mesh axis runs over, the one named last changes fastest.
Arguments:
- video_q: bfloat16 [16, 32, 768, 256], P('tm', 'height'), may hold values from -4.5 to 4.5
- video_k: bfloat16 [16, 32, 768, 256], P('tm', 'height'), may hold values from -4.5 to 4.5
- video_v: bfloat16 [16, 32, 768, 256], P('tm', 'height'), may hold values from -6 to 6
- text_k: bfloat16 [256, 256], P('height'), may hold values from -4.5 to 4.5
- text_v: bfloat16 [256, 256], P('height'), may hold values from -6 to 6
- text_valid: int32 [256], replicated, may hold values from 0 to 1, as said below
- extent: int32 [2, 3], replicated, may hold values from 0 to 1
Outputs:
- video_out: bfloat16 [16, 32, 768, 256], P('tm', 'height')
Inputs may be any that keep to these rules, and one draw needn't show every extreme that they name: `text_valid`: the valid text tokens come first; at least 64 are valid and at least one is not.
All inputs are finite; a program needn't handle non-finite values.
Results may differ from a plain program's by a relative error of at most 0.0042.
Values may be sent and summed in bfloat16 or wider, within the bound.
No kernel may reach another device: no remote copies, remote signals or barrier semaphores. Data moves between devices by JAX's collectives and lax.ppermute only.
A program may use at most 64 MiB of HBM per device.

v0:
```python
import math

import jax
import jax.numpy as jnp
from jax import lax
from jax.sharding import PartitionSpec as P

TILE = 384


def padded_2(array, sides, width):
    for axis, dim in sides:
        size, length = (lax.axis_size(axis), array.shape[dim])
        up = [(i, (i + 1) % size) for i in range(size - 1)]
        down = [(j, i) for i, j in up]
        last = lax.slice_in_dim(array, length - width, length, axis=dim)
        initial = lax.slice_in_dim(array, 0, width, axis=dim)
        before = lax.ppermute(last, axis, up)
        after = lax.ppermute(initial, axis, down)
        array = jnp.concatenate([before, array, after], axis=dim)
    return array


def shards(video_q, video_k, video_v, text_k, text_v, text_valid, extent):
    row_count = video_q.shape[2]
    feat_count = video_q.shape[3]
    head_count = extent.shape[0]
    head_width = feat_count // head_count
    tile_count = row_count // TILE
    score_scale = 1.0 / math.sqrt(head_width)
    key_value = jnp.concatenate((video_k, video_v), axis=3)
    padded = padded_2(key_value, (("tm", 0), ("height", 1)), 1)
    slab_all = padded.reshape(9 * row_count, 2 * feat_count)
    text_keys, text_values = (
        lax.all_gather(text_k, "height", axis=0, tiled=True),
        lax.all_gather(text_v, "height", axis=0, tiled=True),
    )
    time_count = lax.axis_size("tm")
    height_count = lax.axis_size("height")
    local_time = lax.axis_index("tm")
    local_height = lax.axis_index("height")
    key_ids = jnp.arange(9 * row_count, dtype=jnp.int32)
    slab_index = key_ids // row_count
    time_gap = slab_index // 3 - 1
    height_gap = slab_index % 3 - 1
    key_tile = key_ids % row_count // TILE
    inside_keys = (local_time + time_gap >= 0) & (local_time + time_gap < time_count)
    inside_keys = (
        inside_keys & (local_height + height_gap >= 0) & (local_height + height_gap < height_count)
    )
    text_ok = text_valid > 0
    queries = video_q[0, 0].reshape(tile_count, TILE, feat_count)

    def one_block(operands):
        query_block, query_tile = operands
        width_gap = jnp.abs(key_tile - query_tile)
        head_outputs = []
        for head_index in range(head_count):
            low = head_index * head_width
            high = low + head_width
            allowed = (
                inside_keys
                & (jnp.abs(time_gap) <= extent[head_index, 0])
                & (jnp.abs(height_gap) <= extent[head_index, 1])
            )
            allowed = allowed & (width_gap <= extent[head_index, 2])
            query_head = query_block[:, low:high]
            video_scores = (
                jnp.einsum(
                    "qd,kd->qk",
                    query_head,
                    slab_all[:, low:high],
                    preferred_element_type=jnp.float32,
                )
                * score_scale
            )
            text_scores = (
                jnp.einsum(
                    "qd,kd->qk",
                    query_head,
                    text_keys[:, low:high],
                    preferred_element_type=jnp.float32,
                )
                * score_scale
            )
            video_scores = jnp.where(allowed[None, :], video_scores, -jnp.inf)
            text_scores = jnp.where(text_ok[None, :], text_scores, -jnp.inf)
            row_top = jnp.maximum(jnp.max(video_scores, axis=1), jnp.max(text_scores, axis=1))
            video_expo = jnp.exp(video_scores - row_top[:, None])
            text_expo = jnp.exp(text_scores - row_top[:, None])
            row_total = jnp.sum(video_expo, axis=1) + jnp.sum(text_expo, axis=1)
            value_low = feat_count + low
            weighted = jnp.dot(
                video_expo.astype(jnp.bfloat16),
                slab_all[:, value_low : value_low + head_width],
                preferred_element_type=jnp.float32,
            )
            weighted = weighted + jnp.dot(
                text_expo.astype(jnp.bfloat16),
                text_values[:, low:high],
                preferred_element_type=jnp.float32,
            )
            head_outputs.append(weighted / row_total[:, None])
        return jnp.concatenate(head_outputs, axis=1).astype(jnp.bfloat16)

    blocks = lax.map(one_block, (queries, jnp.arange(tile_count, dtype=jnp.int32)))
    return blocks.reshape(video_q.shape)


def solution(mesh):
    return jax.shard_map(
        shards,
        mesh=mesh,
        in_specs=(
            P("tm", "height", None, None),
            P("tm", "height", None, None),
            P("tm", "height", None, None),
            P("height", None),
            P("height", None),
            P(),
            P(),
        ),
        out_specs=P("tm", "height", None, None),
        check_vma=False,
    )
```

profile of v0, /device:TPU:4, one launch (start us, length us, event | category | flops | bytes accessed | tf_op | source)
XLA Modules:
  0.0 332.3 jit_solution(4440091307780463444)
XLA Ops:
  0.0 1.0 constant_dynamic-update-slice_fusion.2
  1.0 1.0 constant_dynamic-update-slice_fusion.1
  2.1 1.9 collective-permute-start
  4.0 3.6 %collective-permute-start.1 = (bf16[1,1,768,512]{3,2,1,0:T(8,128)(2,1)S(1)}, bf16[1,1,768,512]{3,2,1,0:T(8,128)(2,1)S(1)}, u32[]{:S(2)}, u32[]{:S(2)}) collective-permute-start(bf16[1,1,768,512]{3,2,1,0:T(8,128)(2,1)S(1)} %constant_dynamic-update-slice_fusion.1), channel_id=1, source_target_pairs={{32,0},{64,32},{96,64},{128,96},{160,128},{192,160},{224,192},{256... | collective-permute-start | bytes 2359304 | tf_op jit(solution)/shard_map/ppermute | solution.py:19
  7.6 7.7 %collective-permute-done = bf16[1,1,768,512]{3,2,1,0:T(8,128)(2,1)S(1)} collective-permute-done((bf16[1,1,768,512]{3,2,1,0:T(8,128)(2,1)S(1)}, bf16[1,1,768,512]{3,2,1,0:T(8,128)(2,1)S(1)}, u32[]{:S(2)}, u32[]{:S(2)}) %collective-permute-start) | collective-permute-done | bytes 786464 | tf_op jit(solution)/shard_map/ppermute | solution.py:18
  15.4 1.8 collective-permute-done.1
  17.1 1.7 pad_maximum_fusion.2
  18.8 7.5 %collective-permute-start.2 = (bf16[3,1,768,512]{3,2,1,0:T(8,128)(2,1)}, bf16[3,1,768,512]{3,2,1,0:T(8,128)(2,1)}, u32[]{:S(2)}, u32[]{:S(2)}) collective-permute-start(bf16[3,1,768,512]{3,2,1,0:T(8,128)(2,1)} %pad_maximum_fusion.2), channel_id=1, source_target_pairs={{0,1},{1,2},{2,3},{3,4},{4,5},{5,6},{6,7},{7,8},{8,9},{9,10},{10,1... | collective-permute-start | bytes 7077896 | tf_op jit(solution)/shard_map/ppermute | solution.py:18
  26.3 1.3 collective-permute-start.3
  27.6 179.9 %all_gather.6 = bf16[256,256]{1,0:T(8,128)(2,1)S(1)} all-gather(bf16[8,256]{1,0:T(8,128)(2,1)} %param.12), channel_id=1, replica_groups=mesh['tm'=16,'height'=32] {'height'}, dimensions={0}, use_global_device_ids=true | all-gather | bytes 135168 | tf_op jit(solution)/shard_map/all_gather | solution.py:35
  207.5 76.3 %all_gather.7 = bf16[256,256]{1,0:T(8,128)(2,1)S(1)} all-gather(bf16[8,256]{1,0:T(8,128)(2,1)} %param.13), channel_id=1, replica_groups=mesh['tm'=16,'height'=32] {'height'}, dimensions={0}, use_global_device_ids=true | all-gather | bytes 135168 | tf_op jit(solution)/shard_map/all_gather | solution.py:36
  283.7 0.7 broadcast_compare_fusion
  284.4 5.9 %pad_maximum_fusion.1 = bf16[3,3,768,512]{3,2,1,0:T(8,128)(2,1)} fusion(bf16[3,1,768,512]{3,2,1,0:T(8,128)(2,1)} %collective-permute-done.3, bf16[1,1,768,512]{3,2,1,0:T(8,128)(2,1)S(1)} %collective-permute-done.1, bf16[1,1,768,512]{3,2,1,0:T(8,128)(2,1)S(1)} %constant_dynamic-update-slice_fusion.1, bf16[1,1,768,512]{3,2,1,0:T(8,128)(2,1)S(1)} %collective-permute-done, ...), kind=kLoop, calls=%fused_computation.95 | loop fusion | flops 14155776 | bytes 14155776 | tf_op jit(solution)/shard_map/concatenate | solution.py:20
  290.3 41.2 %while.15 = (s32[]{:T(128)}, bf16[2,384,256]{2,1,0:T(8,128)(2,1)S(1)}, s32[2,3]{1,0:T(2,128)S(1)}, s32[2]{0:T(128)S(1)}, bf16[2,384,256]{2,1,0:T(8,128)(2,1)S(1)...) while((s32[]{:T(128)}, ...), condition=%wide.region_9.10_spmd.clone.clone, body=%wide.region_0.9_spmd.clone.clone.sunk | while | flops 2858657792 | bytes 97717000 | solution.py:106
  290.3 0.7 fusion.102
  291.0 0.9 compare_reduce_fusion.10
  292.0 1.0 compare_reduce_fusion.11
  292.9 0.8 compare_reduce_fusion.8
  293.8 1.0 compare_reduce_fusion.9
  294.8 0.6 dynamic_slice.22
  295.3 1.9 compare_and_fusion.4
  297.3 3.3 fusion.109
  300.6 0.2 fusion.110
  300.8 1.6 fusion.112
  302.6 2.0 fusion.111
  304.6 0.2 fusion.114
  304.8 1.7 fusion.103
  306.5 0.2 fusion.104
  306.9 1.6 fusion.106
  308.5 2.0 fusion.105
  310.5 0.2 fusion.108
  311.0 0.7 fusion.102
  311.6 0.9 compare_reduce_fusion.10
  312.6 1.0 compare_reduce_fusion.11
  313.6 0.8 compare_reduce_fusion.8
  314.4 1.0 compare_reduce_fusion.9
  315.4 0.6 dynamic_slice.22
  316.0 1.9 compare_and_fusion.4
  317.9 3.3 fusion.109
  321.2 0.2 fusion.110
  321.5 1.6 fusion.112
  323.2 2.0 fusion.111
  325.2 0.2 fusion.114
  325.5 1.7 fusion.103
  327.1 0.2 fusion.104
  327.5 1.6 fusion.106
  329.1 2.0 fusion.105
  331.6 0.7 copy-done.2
  (40 shorter events, 1.1 us)
Async XLA Ops:
  2.1 13.3 %collective-permute-start = (bf16[1,1,768,512]{3,2,1,0:T(8,128)(2,1)S(1)}, bf16[1,1,768,512]{3,2,1,0:T(8,128)(2,1)S(1)}, u32[]{:S(2)}, u32[]{:S(2)}) collective-permute-start(bf16[1,1,768,512]{3,2,1,0:T(8,128)(2,1)S(1)} %constant_dynamic-update-slice_fusion.1), channel_id=1, source_target_pairs={{0,32},{32,64},{64,96},{96,128},{128,160},{160,192},{192,224},{224... | collective-permute-start | bytes 2359304 | tf_op jit(solution)/shard_map/ppermute | solution.py:18
  4.0 13.1 %collective-permute-start.1 = (bf16[1,1,768,512]{3,2,1,0:T(8,128)(2,1)S(1)}, bf16[1,1,768,512]{3,2,1,0:T(8,128)(2,1)S(1)}, u32[]{:S(2)}, u32[]{:S(2)}) collective-permute-start(bf16[1,1,768,512]{3,2,1,0:T(8,128)(2,1)S(1)} %constant_dynamic-update-slice_fusion.1), channel_id=1, source_target_pairs={{32,0},{64,32},{96,64},{128,96},{160,128},{192,160},{224,192},{256... | collective-permute-start | bytes 2359304 | tf_op jit(solution)/shard_map/ppermute | solution.py:19
  18.8 265.6 %collective-permute-start.2 = (bf16[3,1,768,512]{3,2,1,0:T(8,128)(2,1)}, bf16[3,1,768,512]{3,2,1,0:T(8,128)(2,1)}, u32[]{:S(2)}, u32[]{:S(2)}) collective-permute-start(bf16[3,1,768,512]{3,2,1,0:T(8,128)(2,1)} %pad_maximum_fusion.2), channel_id=1, source_target_pairs={{0,1},{1,2},{2,3},{3,4},{4,5},{5,6},{6,7},{7,8},{8,9},{9,10},{10,1... | collective-permute-start | bytes 7077896 | tf_op jit(solution)/shard_map/ppermute | solution.py:18
  26.3 258.2 %collective-permute-start.3 = (bf16[3,1,768,512]{3,2,1,0:T(8,128)(2,1)}, bf16[3,1,768,512]{3,2,1,0:T(8,128)(2,1)}, u32[]{:S(2)}, u32[]{:S(2)}) collective-permute-start(bf16[3,1,768,512]{3,2,1,0:T(8,128)(2,1)} %pad_maximum_fusion.2), channel_id=1, source_target_pairs={{1,0},{2,1},{3,2},{4,3},{5,4},{6,5},{7,6},{8,7},{9,8},{10,9},{11,1... | collective-permute-start | bytes 7077896 | tf_op jit(solution)/shard_map/ppermute | solution.py:19
  284.4 5.9 %copy-start = (bf16[1,1,768,256]{3,2,1,0:T(8,128)(2,1)S(1)}, bf16[1,1,768,256]{3,2,1,0:T(8,128)(2,1)}, u32[]{:S(2)}) copy-start(bf16[1,1,768,256]{3,2,1,0:T(8,128)(2,1)} %param.9) | copy-start | bytes 1179652
  284.4 5.9 %copy-start.1 = (s32[2,3]{1,0:T(2,128)S(1)}, s32[2,3]{1,0:T(2,128)}, u32[]{:S(2)}) copy-start(s32[2,3]{1,0:T(2,128)} %param.15) | copy-start | bytes 76
  297.3 5.3 %slice-start = ((s8[7077888]{0:T(1024)(128)(4,1)}), s8[4194304]{0:T(1024)(128)(4,1)S(1)}, s32[]{:S(2)}) async-start(s8[7077888]{0:T(1024)(128)(4,1)} %bitcast.37), calls=%async_computation | async-start | bytes 8388608 | tf_op jit(solution)/shard_map/while
  297.3 5.3 %slice-start.1 = ((s8[7077888]{0:T(1024)(128)(4,1)}), s8[2883584]{0:T(1024)(128)(4,1)S(1)}, s32[]{:S(2)}) async-start(s8[7077888]{0:T(1024)(128)(4,1)} %bitcast.37), calls=%async_computation.1 | async-start | bytes 5767168 | tf_op jit(solution)/shard_map/while
  317.9 5.3 %slice-start = ((s8[7077888]{0:T(1024)(128)(4,1)}), s8[4194304]{0:T(1024)(128)(4,1)S(1)}, s32[]{:S(2)}) async-start(s8[7077888]{0:T(1024)(128)(4,1)} %bitcast.37), calls=%async_computation | async-start | bytes 8388608 | tf_op jit(solution)/shard_map/while
  317.9 5.3 %slice-start.1 = ((s8[7077888]{0:T(1024)(128)(4,1)}), s8[2883584]{0:T(1024)(128)(4,1)S(1)}, s32[]{:S(2)}) async-start(s8[7077888]{0:T(1024)(128)(4,1)} %bitcast.37), calls=%async_computation.1 | async-start | bytes 5767168 | tf_op jit(solution)/shard_map/while
  331.6 0.7 copy-start.2
where the time goes:
time: 333 us; the launch traced here: 332 us
  blocking collectives  256 us (77%)
  other arithmetic  26.5 us (8%)
  matrix products  19.8 us (6%)
  starting transfers between devices  14.3 us (4%)
  waiting for transfers between devices  9.49 us (3%)
  local copies, waits for them, and re-layouts  5.73 us (2%)
    all_gather x1, blocking collectives, shards(): lax.all_gather(text_k, 'height', axis=0, tiled=True)  180 us
    all_gather x1, blocking collectives, shards(): lax.all_gather(text_v, 'height', axis=0, tiled=True)  76.3 us
    dot_general x4, matrix products, one_block(): jnp.einsum('qd,kd->qk', query_head, slab_all[:, low:high], preferred_elem...  9.85 us
    ppermute x2, starting transfers between devices, padded_2(): before = lax.ppermute(last, axis, up)  9.4 us
    dot_general x4, matrix products, one_block(): jnp.dot(video_expo.astype(jnp.bfloat16), slab_all[:, value_low:value_low...  7.99 us
    ppermute x2, waiting for transfers between devices, padded_2(): before = lax.ppermute(last, axis, up)  7.73 us
    concatenate x2, other arithmetic, padded_2(): array = jnp.concatenate([before, array, after], axis=dim)  7.55 us
    reduce_sum x8, other arithmetic, one_block(): row_total = jnp.sum(video_expo, axis=1) + jnp.sum(text_expo, axis=1)  6.88 us
  transfers between devices with their start and end apart: 4, of which 2 were waited for; matrix products, arithmetic and copies ran while one was open for 0% of the time, Pallas kernels for 0%

commit v1 on v0

v1 whole, which is shorter than its diff:
```python
import functools
import math

import jax
import jax.numpy as jnp
from jax import lax
from jax.experimental import pallas as pl
from jax.experimental.pallas import tpu as pltpu
from jax.sharding import PartitionSpec as P


TILE = 384
HW = 128
NEG = -1e30
SUB = 128


def rings(axis):
    size = lax.axis_size(axis)
    up = [(i, i + 1) for i in range(size - 1)]
    return up, [(j, i) for i, j in up]


def attention_kernel(spec, *refs):
    jobs, has_own, ends, slabs, n_slab_refs, paired, scale = spec
    refs = list(refs)
    ext_ref, q_ref = refs[:2]
    refs = refs[2:]
    if has_own:
        k_ref, v_ref, text_ref, valid_ref = refs[:4]
        refs = refs[4:]
    else:
        mi_ref, li_ref, ai_ref = refs[:3]
        refs = refs[3:]
    slab_refs = refs[:n_slab_refs]
    refs = refs[n_slab_refs:]
    if ends == "merge":
        other_ref = refs.pop(0)
    if ends == "state":
        mo_ref, lo_ref, ao_ref = refs[:3]
        refs = refs[3:]
    elif ends == "split":
        mo_ref, lo_ref, ao_ref, oo_ref = refs[:4]
        refs = refs[4:]
    else:
        out_ref = refs.pop(0)
    m_ref, l_ref, a_ref = refs
    row_count = q_ref.shape[0]
    tiles = row_count // TILE
    time_at, height_at = lax.axis_index("tm"), lax.axis_index("height")
    height_head = 1 - ext_ref[0, 1]

    def one_tile(step, carry):
        job, w = step // tiles, step % tiles
        head = jnp.where(job == 0, height_head, 1 - height_head)
        low = pl.multiple_of(head * HW, HW)
        wide = ext_ref[head, 2] > 0
        base = pl.multiple_of(w * TILE, TILE)
        rows = pl.ds(base, TILE)

        def attend(k, v, first=False, valid=None):
            for s0 in range(0, TILE, SUB):
                sub = pl.ds(s0, SUB)
                q = q_ref[pl.ds(base + s0, SUB), pl.ds(low, HW)]
                s = lax.dot_general(
                    q, k, (((1,), (1,)), ((), ())), preferred_element_type=jnp.float32
                )
                if valid is not None:
                    s = jnp.where(valid, s, NEG)
                top = jnp.max(s, axis=1, keepdims=True)
                if first:
                    m_new = jnp.broadcast_to(top, (SUB, HW))
                else:
                    m_old = m_ref[sub, :]
                    m_new = jnp.maximum(m_old, top)
                    alpha = jnp.exp2((m_old - m_new) * scale)
                m_ref[sub, :] = m_new
                parts = []
                total = None
                for c in range(0, s.shape[1], HW):
                    p = jnp.exp2((s[:, c : c + HW] - m_new) * scale)
                    total = p if total is None else total + p
                    parts.append(p.astype(jnp.bfloat16))
                p = jnp.concatenate(parts, axis=1)
                pv = jnp.dot(p, v, preferred_element_type=jnp.float32)
                if first:
                    l_ref[sub, :] = total
                    a_ref[sub, :] = pv
                else:
                    l_ref[sub, :] = l_ref[sub, :] * alpha + total
                    a_ref[sub, :] = a_ref[sub, :] * alpha + pv

        def slab(kr, vr, row0, kc, vc, first=False):
            @pl.when(wide)
            def _():
                at = pl.ds(pl.multiple_of(row0, TILE), row_count)
                attend(kr[at, pl.ds(kc, HW)], vr[at, pl.ds(vc, HW)], first)

            @pl.when(jnp.logical_not(wide))
            def _():
                at = pl.ds(pl.multiple_of(row0 + base, TILE), TILE)
                attend(kr[at, pl.ds(kc, HW)], vr[at, pl.ds(vc, HW)], first)

        if has_own:
            slab(k_ref, v_ref, 0, low, low, True)
            attend(
                text_ref[:, pl.ds(low, HW)],
                text_ref[:, pl.ds(pl.multiple_of(low + 2 * HW, HW), HW)],
                valid=valid_ref[...] > 0,
            )
        else:
            m_ref[...] = mi_ref[rows, :]
            l_ref[...] = li_ref[rows, :]
            a_ref[...] = ai_ref[rows, :]

        for ref_id, count, dt, dh in slabs:
            ref = slab_refs[ref_id]
            kc = low if paired else 0
            vc = pl.multiple_of(low + 2 * HW, HW) if paired else HW

            def one_slab(i, carry, ref=ref, dt=dt, dh=dh, kc=kc, vc=vc):
                time, height = time_at + dt, height_at + dh + i
                held = (time >= 0) & (time < lax.axis_size("tm"))
                held = held & (height >= 0) & (height < lax.axis_size("height"))
                if dt != 0:
                    held = held & (ext_ref[head, 0] > 0)
                held = held & (jnp.abs(dh + i) <= ext_ref[head, 1])

                @pl.when(held)
                def _():
                    slab(ref, ref, i * row_count, kc, vc)

                return carry

            if count == 1:
                one_slab(0, 0)
            else:
                lax.fori_loop(0, count, one_slab, 0)

        def keep():
            mo_ref[rows, :] = m_ref[...]
            lo_ref[rows, :] = l_ref[...]
            ao_ref[rows, :] = a_ref[...]

        def finish(ref, cols):
            total = jnp.sum(l_ref[...], axis=1, keepdims=True)
            ref[rows, cols] = (a_ref[...] / total).astype(jnp.bfloat16)

        if ends == "state":
            keep()
        elif ends == "split":
            pl.when(job == 0)(keep)
            pl.when(job != 0)(lambda: finish(oo_ref, pl.ds(0, HW)))
        else:
            finish(out_ref, pl.ds(low, HW))
            if ends == "merge":
                cols = pl.ds(pl.multiple_of((1 - head) * HW, HW), HW)
                out_ref[rows, cols] = other_ref[rows, :]
        return carry

    lax.fori_loop(0, jobs * tiles, one_tile, 0)


SMEM = pl.BlockSpec(memory_space=pltpu.SMEM)
VMEM = pl.BlockSpec(memory_space=pltpu.VMEM)


def attention(jobs, ends, slabs, ext, q, arrays, own=None, state=None, other=None, paired=False):
    rows, feat = q.shape
    scale = math.log2(math.e) / math.sqrt(HW)
    spec = (jobs, own is not None, ends, slabs, len(arrays), paired, scale)
    args = [ext, q] + list(own if own is not None else state) + list(arrays)
    if other is not None:
        args.append(other)
    part = jax.ShapeDtypeStruct((rows, HW), jnp.float32)
    if ends == "state":
        outs = (part,) * 3
    elif ends == "split":
        outs = (part,) * 3 + (jax.ShapeDtypeStruct((rows, HW), jnp.bfloat16),)
    else:
        outs = jax.ShapeDtypeStruct((rows, feat), jnp.bfloat16)
    scores = rows * rows * (sum(s[1] for s in slabs) + 1)
    return pl.pallas_call(
        functools.partial(attention_kernel, spec),
        out_shape=outs,
        in_specs=[SMEM] + [VMEM] * (len(args) - 1),
        out_specs=(VMEM,) * len(outs) if isinstance(outs, tuple) else VMEM,
        scratch_shapes=[pltpu.VMEM((TILE, HW), jnp.float32)] * 3,
        compiler_params=pltpu.CompilerParams(vmem_limit_bytes=40 * 1024 * 1024),
        cost_estimate=pl.CostEstimate(
            flops=4 * HW * scores, bytes_accessed=4 * rows * feat * 4, transcendentals=scores
        ),
    )(*args)


def pick_kernel(ext_ref, k_ref, v_ref, out_ref):
    out_ref[:, :HW] = k_ref[...]
    out_ref[:, HW:] = v_ref[...]


def of_head(ext, k, v, axis):
    rows = k.shape[0]
    part = pl.BlockSpec((rows, HW), lambda i, ext_ref: (0, 1 - ext_ref[0, axis]))
    return pl.pallas_call(
        pick_kernel,
        grid_spec=pltpu.PrefetchScalarGridSpec(
            num_scalar_prefetch=1,
            grid=(1,),
            in_specs=[part, part],
            out_specs=pl.BlockSpec((rows, 2 * HW), lambda i, ext_ref: (0, 0)),
        ),
        out_shape=jax.ShapeDtypeStruct((rows, 2 * HW), k.dtype),
        cost_estimate=pl.CostEstimate(flops=0, bytes_accessed=8 * rows * HW, transcendentals=0),
    )(ext, k, v)


def shards(video_q, video_k, video_v, text_k, text_v, text_valid, extent):
    rows, feat = video_q.shape[2:]
    q, k, v = (a.reshape(rows, feat) for a in (video_q, video_k, video_v))
    hn = lax.axis_size("height")
    t_rings, h_rings = rings("tm"), rings("height")
    valid = text_valid.reshape(1, -1)

    table = 0
    for c in range(16):
        t0, h0, t1, h1 = (c >> i & 1 for i in range(4))
        crowded = (t0 and t1) or (h0 and h1)
        table |= (2 if crowded else int((t0 and h0) or (t1 and h1))) << (2 * c)
    table -= (table >> 31) << 32
    shift = jnp.sum(extent * jnp.array([[2, 4, 0], [8, 16, 0]], jnp.int32))
    branch = lax.shift_right_arithmetic(jnp.int32(table), shift) & 3

    def text_tokens(text_k, text_v):
        mine = jnp.concatenate([text_k, text_v], axis=1)
        copies = jnp.broadcast_to(mine[None], (hn,) + mine.shape)
        got = lax.all_to_all(copies, "height", 0, 0)
        return got.reshape(-1, mine.shape[1])

    def exchange(x, axis, pairs):
        up, down = pairs
        before = lax.ppermute(x, axis, up)
        after = lax.ppermute(x, axis, down)
        return before, after

    def sparse(diagonal):
        def run(q, k, v, text_k, text_v, valid, ext):
            kv_h = of_head(ext, k, v, 1)
            h0, h1 = exchange(kv_h, "height", h_rings)
            kv_t = of_head(ext, k, v, 0)
            t0, t1 = exchange(kv_t, "tm", t_rings)
            text = text_tokens(text_k, text_v)
            m, l, a, other = attention(
                2, "split", ((0, 1, -1, 0), (1, 1, 1, 0)),
                ext, q, (t0, t1), own=(k, v, text, valid),
            )
            hs = ((0, 1, 0, -1), (1, 1, 0, 1))
            if not diagonal:
                return attention(1, "merge", hs, ext, q, (h0, h1), state=(m, l, a), other=other)
            d00, d10 = exchange(h0, "tm", t_rings)
            d01, d11 = exchange(h1, "tm", t_rings)
            m, l, a = attention(1, "state", hs, ext, q, (h0, h1), state=(m, l, a))
            ds = ((0, 1, -1, -1), (1, 1, 1, -1), (2, 1, -1, 1), (3, 1, 1, 1))
            return attention(
                1, "merge", ds, ext, q, (d00, d10, d01, d11),
                state=(m, l, a), other=other,
            )

        return run

    def dense(q, k, v, text_k, text_v, valid, ext):
        kv = jnp.concatenate([k, v], axis=1)
        h0, h1 = exchange(kv, "height", h_rings)
        text = text_tokens(text_k, text_v)
        three = jnp.concatenate([h0, kv, h1], axis=0)
        t0, t1 = exchange(three, "tm", t_rings)
        slabs = ((0, 1, 0, -1), (1, 1, 0, 1), (2, 3, -1, -1), (3, 3, 1, -1))
        return attention(
            2, "all", slabs, ext, q, (h0, h1, t0, t1),
            own=(k, v, text, valid), paired=True,
        )

    out = lax.switch(
        branch, [sparse(False), sparse(True), dense], q, k, v, text_k, text_v, valid, extent
    )
    return out.reshape(video_q.shape)


def solution(mesh):
    video = P("tm", "height", None, None)
    return jax.shard_map(
        shards,
        mesh=mesh,
        in_specs=(video, video, video, P("height", None), P("height", None), P(), P()),
        out_specs=video,
        check_vma=False,
    )
```

time: 333 us -> 81.2 us (0.24)
  the two profiles are of different devices: /device:TPU:4 before, /device:TPU:38 now
where the time goes in v1:
time: 81.2 us; the launch traced here: 80.7 us
  starting transfers between devices  40.1 us (49%)
  Pallas kernels  30.4 us (37%)
  waiting for transfers between devices  5.93 us (7%)
  local copies, waits for them, and re-layouts  1.49 us (2%)
  other arithmetic  1.34 us (2%)
    pallas_call x3, Pallas kernels, attention(): pl.pallas_call(functools.partial(attention_kernel, spec), out_shape=outs,...  25.2 us
    ppermute x4, starting transfers between devices, exchange(): after = lax.ppermute(x, axis, down)  17.3 us
    ppermute x4, starting transfers between devices, exchange(): before = lax.ppermute(x, axis, up)  11.8 us
    all_to_all x1, starting transfers between devices, text_tokens(): got = lax.all_to_all(copies, 'height', 0, 0)  11 us
    ppermute x4, waiting for transfers between devices, exchange(): after = lax.ppermute(x, axis, down)  5.91 us
    pallas_call x2, Pallas kernels, of_head(): pl.pallas_call(pick_kernel, grid_spec=pltpu.PrefetchScalarGridSpec(num_sc...  5.18 us
  transfers between devices with their start and end apart: 9, of which 1 were waited for; matrix products, arithmetic and copies ran while one was open for 1% of the time, Pallas kernels for 24%

profile of v1, /device:TPU:38, one launch (start us, length us, event | category | flops | bytes accessed | tf_op | source)
XLA Modules:
  0.0 80.7 jit_solution(18155210495579439248)
XLA Ops:
  0.0 1.3 %multiply_reduce_fusion = s32[]{:T(128)} fusion(s32[2,3]{1,0:T(2,128)} %param.17, s32[2,3]{1,0:T(2,128)} %constant.10.clone), kind=kLoop, calls=%fused_computation.6 | loop fusion | flops 11 | bytes 52 | tf_op jit(solution)/shard_map/reduce_sum | solution.py:230
  2.0 77.9 %conditional.1 = (bf16[1,1,768,256]{3,2,1,0:T(8,128)(2,1)S(1)}) conditional(s32[]{:T(128)} %clamp.3, (bf16[8,256]{1,0:T(8,128)(2,1)}, bf16[8,256]{1,0:T(8,128)(2,1)}, s32[2,3]{1,0:T(2,128)}, bf16[768,256]{1,0:T(8,128)(2,1)}, bf16[768,256]{1,0:T(8,128)(2,1)}, /*index=5*/bf16[768,256]{1,0:T(8,128)(2,1)}, ...), branch_computations={%region_1.0_spmd, %region_2.0_spmd, %region_3.0_spmd} | conditional | flops 3321905152 | bytes 40169932 | solution.py:282
  2.0 0.0 copy-start.4
  2.0 0.0 copy-start.6
  2.0 0.0 copy-start.9
  2.0 0.0 copy-start.15
  2.1 2.7 %branch_1_fun.7 = bf16[768,256]{1,0:T(8,128)(2,1)} custom-call(s32[2,3]{1,0:T(2,128)} %get-tuple-element.63.ext_ref.refs_0_, bf16[768,256]{1,0:T(8,128)(2,1)} %get-tuple-element.65.k_ref.refs_2_, bf16[768,256]{1,0:T(8,128)(2,1)} %get-tuple-element.66.v_ref.refs_3_), custom_call_target="tpu_custom_call" | custom-call | bytes 786432 | tf_op jit(solution)/shard_map/cond/branch_1_fun/pallas_call | solution.py:204
  4.7 6.1 %collective-permute-start.6 = (bf16[768,256]{1,0:T(8,128)(2,1)}, bf16[768,256]{1,0:T(8,128)(2,1)S(1)}, u32[]{:S(2)}, u32[]{:S(2)}) collective-permute-start(bf16[768,256]{1,0:T(8,128)(2,1)} %branch_1_fun.7), channel_id=1, source_target_pairs={{0,1},{1,2},{2,3},{3,4},{4,5},{5,6},{6,7},{7,8},{8,9},{9,10},{10,1... | collective-permute-start | bytes 1179656 | tf_op jit(solution)/shard_map/cond/branch_1_fun/ppermute | solution.py:241
  10.8 6.7 %collective-permute-start.7 = (bf16[768,256]{1,0:T(8,128)(2,1)}, bf16[768,256]{1,0:T(8,128)(2,1)S(1)}, u32[]{:S(2)}, u32[]{:S(2)}) collective-permute-start(bf16[768,256]{1,0:T(8,128)(2,1)} %branch_1_fun.7), channel_id=1, source_target_pairs={{1,0},{2,1},{3,2},{4,3},{5,4},{6,5},{7,6},{8,7},{9,8},{10,9},{11,1... | collective-permute-start | bytes 1179656 | tf_op jit(solution)/shard_map/cond/branch_1_fun/ppermute | solution.py:242
  17.5 2.5 %branch_1_fun.5 = bf16[768,256]{1,0:T(8,128)(2,1)} custom-call(s32[2,3]{1,0:T(2,128)} %get-tuple-element.63.ext_ref.refs_0_, bf16[768,256]{1,0:T(8,128)(2,1)} %get-tuple-element.65.k_ref.refs_2_, bf16[768,256]{1,0:T(8,128)(2,1)} %get-tuple-element.66.v_ref.refs_3_), custom_call_target="tpu_custom_call" | custom-call | bytes 786432 | tf_op jit(solution)/shard_map/cond/branch_1_fun/pallas_call | solution.py:204
  20.0 1.9 %collective-permute-start.4 = (bf16[768,256]{1,0:T(8,128)(2,1)}, bf16[768,256]{1,0:T(8,128)(2,1)S(1)}, u32[]{:S(2)}, u32[]{:S(2)}) collective-permute-start(bf16[768,256]{1,0:T(8,128)(2,1)} %branch_1_fun.5), channel_id=1, source_target_pairs={{0,32},{32,64},{64,96},{96,128},{128,160},{160,192},{192,224},{224... | collective-permute-start | bytes 1179656 | tf_op jit(solution)/shard_map/cond/branch_1_fun/ppermute | solution.py:241
  21.9 0.0 copy-done.4
  21.9 0.0 copy-done.6
  21.9 0.7 broadcast_in_dim.8
  22.7 11.0 %all-to-all-start.1 = ((bf16[32,8,512]{2,1,0:T(8,128)(2,1)}), bf16[32,8,512]{2,1,0:T(8,128)(2,1)S(1)}, u32[]{:S(2)}, u32[]{:S(2)}) async-start(bf16[32,8,512]{2,1,0:T(8,128)(2,1)} %broadcast_in_dim.8), calls=%async_computation.1 | async-start | bytes 524288 | tf_op jit(solution)/shard_map/cond/branch_1_fun/all_to_all | solution.py:236
  33.7 3.1 %collective-permute-start.5 = (bf16[768,256]{1,0:T(8,128)(2,1)}, bf16[768,256]{1,0:T(8,128)(2,1)S(1)}, u32[]{:S(2)}, u32[]{:S(2)}) collective-permute-start(bf16[768,256]{1,0:T(8,128)(2,1)} %branch_1_fun.5), channel_id=1, source_target_pairs={{32,0},{64,32},{96,64},{128,96},{160,128},{192,160},{224,192},{256... | collective-permute-start | bytes 1179656 | tf_op jit(solution)/shard_map/cond/branch_1_fun/ppermute | solution.py:242
  36.8 5.9 %collective-permute-done.7.refs_6_ = bf16[768,256]{1,0:T(8,128)(2,1)S(1)} collective-permute-done((bf16[768,256]{1,0:T(8,128)(2,1)}, bf16[768,256]{1,0:T(8,128)(2,1)S(1)}, u32[]{:S(2)}, u32[]{:S(2)}) %collective-permute-start.7) | collective-permute-done | bytes 393248 | tf_op jit(solution)/shard_map/cond/branch_1_fun/ppermute | solution.py:242
  42.7 1.9 %collective-permute-start.10 = (bf16[768,256]{1,0:T(8,128)(2,1)S(1)}, bf16[768,256]{1,0:T(8,128)(2,1)S(1)}, u32[]{:S(2)}, u32[]{:S(2)}) collective-permute-start(bf16[768,256]{1,0:T(8,128)(2,1)S(1)} %collective-permute-done.7.refs_6_), channel_id=1, source_target_pairs={{0,32},{32,64},{64,96},{96,128},{128,160},{160,192},{192,224},{224... | collective-permute-start | bytes 1179656 | tf_op jit(solution)/shard_map/cond/branch_1_fun/ppermute | solution.py:241
  44.6 3.6 %collective-permute-start.11 = (bf16[768,256]{1,0:T(8,128)(2,1)S(1)}, bf16[768,256]{1,0:T(8,128)(2,1)S(1)}, u32[]{:S(2)}, u32[]{:S(2)}) collective-permute-start(bf16[768,256]{1,0:T(8,128)(2,1)S(1)} %collective-permute-done.7.refs_6_), channel_id=1, source_target_pairs={{32,0},{64,32},{96,64},{128,96},{160,128},{192,160},{224,192},{256... | collective-permute-start | bytes 1179656 | tf_op jit(solution)/shard_map/cond/branch_1_fun/ppermute | solution.py:242
  48.3 0.0 collective-permute-done.6.refs_5_
  48.3 1.9 %collective-permute-start.8 = (bf16[768,256]{1,0:T(8,128)(2,1)S(1)}, bf16[768,256]{1,0:T(8,128)(2,1)S(1)}, u32[]{:S(2)}, u32[]{:S(2)}) collective-permute-start(bf16[768,256]{1,0:T(8,128)(2,1)S(1)} %collective-permute-done.6.refs_5_), channel_id=1, source_target_pairs={{0,32},{32,64},{64,96},{96,128},{128,160},{160,192},{192,224},{224... | collective-permute-start | bytes 1179656 | tf_op jit(solution)/shard_map/cond/branch_1_fun/ppermute | solution.py:241
  50.2 0.0 collective-permute-done.4.refs_6_
  50.2 3.9 %collective-permute-start.9 = (bf16[768,256]{1,0:T(8,128)(2,1)S(1)}, bf16[768,256]{1,0:T(8,128)(2,1)S(1)}, u32[]{:S(2)}, u32[]{:S(2)}) collective-permute-start(bf16[768,256]{1,0:T(8,128)(2,1)S(1)} %collective-permute-done.6.refs_5_), channel_id=1, source_target_pairs={{32,0},{64,32},{96,64},{128,96},{160,128},{192,160},{224,192},{256... | collective-permute-start | bytes 1179656 | tf_op jit(solution)/shard_map/cond/branch_1_fun/ppermute | solution.py:242
  54.1 0.0 collective-permute-done.5.refs_7_
  54.1 0.0 all-to-all-done.1
  54.1 0.0 copy-start.12
  54.1 0.0 copy-done.9
  54.1 0.0 copy-done.15
  54.1 12.2 %branch_1_fun.6 = (f32[768,128]{1,0:T(8,128)S(1)}, f32[768,128]{1,0:T(8,128)S(1)}, f32[768,128]{1,0:T(8,128)S(1)}, bf16[768,128]{1,0:T(8,128)(2,1)S(1)}) custom-call(s32[2,3]{1,0:T(2,128)S(1)} %copy-done.9, bf16[768,256]{1,0:T(8,128)(2,1)} %get-tuple-element.64.refs_1_, bf16[768,256]{1,0:T(8,128)(2,1)} %get-tuple-element.65.k_ref.refs_2_, ...), custom_call_target="tpu_custom_call" | custom-call | flops 905969664 | bytes 3145728 | tf_op jit(solution)/shard_map/cond/branch_1_fun/pallas_call | solution.py:183
  66.4 0.0 copy-done.12
  66.4 4.5 %branch_1_fun.8 = (f32[768,128]{1,0:T(8,128)S(1)}, f32[768,128]{1,0:T(8,128)S(1)}, f32[768,128]{1,0:T(8,128)S(1)}) custom-call(s32[2,3]{1,0:T(2,128)S(1)} %copy-done.9, bf16[768,256]{1,0:T(8,128)(2,1)S(1)} %copy-done.12, f32[768,128]{1,0:T(8,128)S(1)} %get-tuple-element.70.refs_2_, f32[768,128]{1,0:T(8,128)S(1)} %get-tuple-element.71.refs_3_, ...), custom_call_target="tpu_custom_call" | custom-call | flops 905969664 | bytes 3145728 | tf_op jit(solution)/shard_map/cond/branch_1_fun/pallas_call | solution.py:183
  70.9 0.0 collective-permute-done.10.refs_7_
  70.9 0.0 collective-permute-done.11.refs_8_
  70.9 0.0 collective-permute-done.8.refs_5_
  70.9 0.0 collective-permute-done.9.refs_6_
  70.9 8.5 %branch_1_fun.9 = bf16[768,256]{1,0:T(8,128)(2,1)S(1)} custom-call(s32[2,3]{1,0:T(2,128)S(1)} %copy-done.9, bf16[768,256]{1,0:T(8,128)(2,1)S(1)} %copy-done.12, f32[768,128]{1,0:T(8,128)S(1)} %get-tuple-element.73.refs_2_, f32[768,128]{1,0:T(8,128)S(1)} %get-tuple-element.74.refs_3_, f32[768,128]{1,0:T(8,128)S(1)} %get-tuple-element.75.refs_4_, ...), custom_call_target="tpu_custom_call" | custom-call | flops 1509949440 | bytes 3145728 | tf_op jit(solution)/shard_map/cond/branch_1_fun/pallas_call | solution.py:183
  79.9 0.0 copy-start.17
  79.9 0.7 copy-done.17
  (1 shorter events, 0.0 us)
Async XLA Ops:
  2.0 19.9 %copy-start.4 = (bf16[8,256]{1,0:T(8,128)(2,1)S(1)}, bf16[8,256]{1,0:T(8,128)(2,1)}, u32[]{:S(2)}) copy-start(bf16[8,256]{1,0:T(8,128)(2,1)} %get-tuple-element.67) | copy-start | bytes 12292 | tf_op jit(solution)/shard_map/cond
  2.0 19.9 %copy-start.6 = (bf16[8,256]{1,0:T(8,128)(2,1)S(1)}, bf16[8,256]{1,0:T(8,128)(2,1)}, u32[]{:S(2)}) copy-start(bf16[8,256]{1,0:T(8,128)(2,1)} %get-tuple-element.68) | copy-start | bytes 12292 | tf_op jit(solution)/shard_map/cond
  2.0 52.1 %copy-start.9 = (s32[2,3]{1,0:T(2,128)S(1)}, s32[2,3]{1,0:T(2,128)}, u32[]{:S(2)}) copy-start(s32[2,3]{1,0:T(2,128)} %get-tuple-element.63.ext_ref.refs_0_) | copy-start | bytes 76 | tf_op jit(solution)/shard_map/cond
  2.0 52.1 %copy-start.15 = (s32[1,256]{1,0:T(1,128)S(1)}, s32[1,256]{1,0:T(1,128)}, u32[]{:S(2)}) copy-start(s32[1,256]{1,0:T(1,128)} %get-tuple-element.69.refs_5_) | copy-start | bytes 3076 | tf_op jit(solution)/shard_map/cond
  4.7 43.5 %collective-permute-start.6 = (bf16[768,256]{1,0:T(8,128)(2,1)}, bf16[768,256]{1,0:T(8,128)(2,1)S(1)}, u32[]{:S(2)}, u32[]{:S(2)}) collective-permute-start(bf16[768,256]{1,0:T(8,128)(2,1)} %branch_1_fun.7), channel_id=1, source_target_pairs={{0,1},{1,2},{2,3},{3,4},{4,5},{5,6},{6,7},{7,8},{8,9},{9,10},{10,1... | collective-permute-start | bytes 1179656 | tf_op jit(solution)/shard_map/cond/branch_1_fun/ppermute | solution.py:241
  10.8 31.9 %collective-permute-start.7 = (bf16[768,256]{1,0:T(8,128)(2,1)}, bf16[768,256]{1,0:T(8,128)(2,1)S(1)}, u32[]{:S(2)}, u32[]{:S(2)}) collective-permute-start(bf16[768,256]{1,0:T(8,128)(2,1)} %branch_1_fun.7), channel_id=1, source_target_pairs={{1,0},{2,1},{3,2},{4,3},{5,4},{6,5},{7,6},{8,7},{9,8},{10,9},{11,1... | collective-permute-start | bytes 1179656 | tf_op jit(solution)/shard_map/cond/branch_1_fun/ppermute | solution.py:242
  20.0 30.2 %collective-permute-start.4 = (bf16[768,256]{1,0:T(8,128)(2,1)}, bf16[768,256]{1,0:T(8,128)(2,1)S(1)}, u32[]{:S(2)}, u32[]{:S(2)}) collective-permute-start(bf16[768,256]{1,0:T(8,128)(2,1)} %branch_1_fun.5), channel_id=1, source_target_pairs={{0,32},{32,64},{64,96},{96,128},{128,160},{160,192},{192,224},{224... | collective-permute-start | bytes 1179656 | tf_op jit(solution)/shard_map/cond/branch_1_fun/ppermute | solution.py:241
  22.7 31.4 %all-to-all-start.1 = ((bf16[32,8,512]{2,1,0:T(8,128)(2,1)}), bf16[32,8,512]{2,1,0:T(8,128)(2,1)S(1)}, u32[]{:S(2)}, u32[]{:S(2)}) async-start(bf16[32,8,512]{2,1,0:T(8,128)(2,1)} %broadcast_in_dim.8), calls=%async_computation.1 | async-start | bytes 524288 | tf_op jit(solution)/shard_map/cond/branch_1_fun/all_to_all | solution.py:236
  33.7 20.4 %collective-permute-start.5 = (bf16[768,256]{1,0:T(8,128)(2,1)}, bf16[768,256]{1,0:T(8,128)(2,1)S(1)}, u32[]{:S(2)}, u32[]{:S(2)}) collective-permute-start(bf16[768,256]{1,0:T(8,128)(2,1)} %branch_1_fun.5), channel_id=1, source_target_pairs={{32,0},{64,32},{96,64},{128,96},{160,128},{192,160},{224,192},{256... | collective-permute-start | bytes 1179656 | tf_op jit(solution)/shard_map/cond/branch_1_fun/ppermute | solution.py:242
  42.7 28.2 %collective-permute-start.10 = (bf16[768,256]{1,0:T(8,128)(2,1)S(1)}, bf16[768,256]{1,0:T(8,128)(2,1)S(1)}, u32[]{:S(2)}, u32[]{:S(2)}) collective-permute-start(bf16[768,256]{1,0:T(8,128)(2,1)S(1)} %collective-permute-done.7.refs_6_), channel_id=1, source_target_pairs={{0,32},{32,64},{64,96},{96,128},{128,160},{160,192},{192,224},{224... | collective-permute-start | bytes 1179656 | tf_op jit(solution)/shard_map/cond/branch_1_fun/ppermute | solution.py:241
  44.6 26.3 %collective-permute-start.11 = (bf16[768,256]{1,0:T(8,128)(2,1)S(1)}, bf16[768,256]{1,0:T(8,128)(2,1)S(1)}, u32[]{:S(2)}, u32[]{:S(2)}) collective-permute-start(bf16[768,256]{1,0:T(8,128)(2,1)S(1)} %collective-permute-done.7.refs_6_), channel_id=1, source_target_pairs={{32,0},{64,32},{96,64},{128,96},{160,128},{192,160},{224,192},{256... | collective-permute-start | bytes 1179656 | tf_op jit(solution)/shard_map/cond/branch_1_fun/ppermute | solution.py:242
  48.3 22.7 %collective-permute-start.8 = (bf16[768,256]{1,0:T(8,128)(2,1)S(1)}, bf16[768,256]{1,0:T(8,128)(2,1)S(1)}, u32[]{:S(2)}, u32[]{:S(2)}) collective-permute-start(bf16[768,256]{1,0:T(8,128)(2,1)S(1)} %collective-permute-done.6.refs_5_), channel_id=1, source_target_pairs={{0,32},{32,64},{64,96},{96,128},{128,160},{160,192},{192,224},{224... | collective-permute-start | bytes 1179656 | tf_op jit(solution)/shard_map/cond/branch_1_fun/ppermute | solution.py:241
  50.2 20.7 %collective-permute-start.9 = (bf16[768,256]{1,0:T(8,128)(2,1)S(1)}, bf16[768,256]{1,0:T(8,128)(2,1)S(1)}, u32[]{:S(2)}, u32[]{:S(2)}) collective-permute-start(bf16[768,256]{1,0:T(8,128)(2,1)S(1)} %collective-permute-done.6.refs_5_), channel_id=1, source_target_pairs={{32,0},{64,32},{96,64},{128,96},{160,128},{192,160},{224,192},{256... | collective-permute-start | bytes 1179656 | tf_op jit(solution)/shard_map/cond/branch_1_fun/ppermute | solution.py:242
  54.1 12.3 %copy-start.12 = (bf16[768,256]{1,0:T(8,128)(2,1)S(1)}, bf16[768,256]{1,0:T(8,128)(2,1)}, u32[]{:S(2)}) copy-start(bf16[768,256]{1,0:T(8,128)(2,1)} %get-tuple-element.64.refs_1_) | copy-start | bytes 1179652 | tf_op jit(solution)/shard_map/cond
  79.9 0.7 copy-start.17

commit v2 on v1

v2 whole, which is shorter than its diff:
```python
import functools
import math

import jax
import jax.numpy as jnp
from jax import lax
from jax.experimental import pallas as pl
from jax.experimental.pallas import tpu as pltpu
from jax.sharding import PartitionSpec as P


TILE = 384
HW = 128
NEG = -1e30
MARK = 1e30
SLOW = 128


def rings(axis):
    size = lax.axis_size(axis)
    up = [(i, i + 1) for i in range(size - 1)]
    return up, [(j, i) for i, j in up]


def attention_kernel(spec, *refs):
    jobs, has_own, ends, slabs, n_slab_refs, paired, scale = spec
    refs = list(refs)
    ext_ref, q_ref = refs[:2]
    refs = refs[2:]
    if has_own:
        k_ref, v_ref, text_ref, valid_ref = refs[:4]
        refs = refs[4:]
    else:
        mi_ref, li_ref, ai_ref = refs[:3]
        refs = refs[3:]
    slab_refs = refs[:n_slab_refs]
    refs = refs[n_slab_refs:]
    if ends == "merge":
        other_ref = refs.pop(0)
    if ends == "state":
        mo_ref, lo_ref, ao_ref = refs[:3]
        refs = refs[3:]
    elif ends == "split":
        mo_ref, lo_ref, ao_ref, oo_ref = refs[:4]
        refs = refs[4:]
    else:
        out_ref = refs.pop(0)
    m_ref, l_ref, a_ref = refs
    row_count = q_ref.shape[0]
    tiles = row_count // TILE
    time_at, height_at = lax.axis_index("tm"), lax.axis_index("height")
    height_head = 1 - ext_ref[0, 1]
    compact = ends == "all"

    def reaches(head, along_time, along_height):
        needed = jnp.bool_(True)
        if along_time:
            needed = needed & (ext_ref[head, 0] > 0)
        if along_height:
            needed = needed & (ext_ref[head, 1] > 0)
        return needed

    def one_head(job, carry):
        head = jnp.where(job == 0, height_head, 1 - height_head)
        low = pl.multiple_of(head * HW, HW)
        high = pl.multiple_of(low + 2 * HW, HW)
        wide = ext_ref[head, 2] > 0
        q_cols = pl.ds(low, HW)

        def fast(row, count, k, v, held=None, valid=None, base=(l_ref, a_ref)):
            at = pl.ds(row, count)
            s = lax.dot_general(
                q_ref[at, q_cols], k, (((1,), (1,)), ((), ())),
                preferred_element_type=jnp.float32,
            )
            parts = []
            total = None
            for c in range(0, s.shape[1], HW):
                p = jnp.exp2(s[:, c : c + HW] * scale)
                if valid is not None:
                    p = jnp.where(valid[:, c : c + HW], p, 0.0)
                total = p if total is None else total + p
                parts.append(p.astype(jnp.bfloat16))
            if held is not None:
                total = total * held
            pv = jnp.dot(
                jnp.concatenate(parts, axis=1), v, preferred_element_type=jnp.float32
            )
            l_ref[at, :] = total if base is None else base[0][at, :] + total
            a_ref[at, :] = pv if base is None else base[1][at, :] + pv

        def slow(row, k, v, valid=None):
            def one_sub(i, carry):
                sub = pl.ds(pl.multiple_of(row + i * SLOW, SLOW), SLOW)
                s = lax.dot_general(
                    q_ref[sub, q_cols], k, (((1,), (1,)), ((), ())),
                    preferred_element_type=jnp.float32,
                )
                if valid is not None:
                    s = jnp.where(valid, s, NEG)
                m_old = m_ref[sub, :]
                m_new = jnp.maximum(m_old, jnp.max(s, axis=1, keepdims=True))
                alpha = jnp.exp2((m_old - m_new) * scale)
                p = jnp.exp2((s - m_new[:, :1]) * scale)
                total = sum(p[:, c : c + HW] for c in range(0, s.shape[1], HW))
                m_ref[sub, :] = m_new
                l_ref[sub, :] = l_ref[sub, :] * alpha + total
                a_ref[sub, :] = a_ref[sub, :] * alpha + jnp.dot(
                    p.astype(jnp.bfloat16), v, preferred_element_type=jnp.float32
                )
                return carry

            lax.fori_loop(0, TILE // SLOW, one_sub, 0)

        if has_own:
            reach = jnp.abs(q_ref[:, q_cols].astype(jnp.float32))
            safe = jnp.max(jnp.sum(reach, axis=1, keepdims=True)) * (4.5 * scale) < 90.0
        else:
            safe = mi_ref[0, 0] > MARK / 2
        unsafe = jnp.logical_not(safe)

        def group(needed, members, base=(l_ref, a_ref)):
            def whole(row, count, shift):
                start = base
                for kr, vr, row0, kc, vc, held in members:
                    at = pl.ds(row0 + shift, count)
                    held = None if held is None else held.astype(jnp.float32)
                    k, v = kr[at, pl.ds(kc, HW)], vr[at, pl.ds(vc, HW)]
                    fast(row, count, k, v, held, base=start)
                    start = (l_ref, a_ref)

            def one_pair(i, carry):
                w, w2 = i // tiles, i % tiles
                row = pl.multiple_of(w * TILE, TILE)
                for kr, vr, row0, kc, vc, held in members:
                    seen = wide | (w2 == w)
                    seen = seen if held is None else seen & (held > 0)
                    at = pl.ds(pl.multiple_of(row0 + w2 * TILE, TILE), TILE)

                    @pl.when(seen & unsafe)
                    def _(kr=kr, vr=vr, at=at, kc=kc, vc=vc):
                        slow(row, kr[at, pl.ds(kc, HW)], vr[at, pl.ds(vc, HW)])

                    if compact:

                        @pl.when(seen & safe)
                        def _(kr=kr, vr=vr, at=at, kc=kc, vc=vc):
                            fast(row, TILE, kr[at, pl.ds(kc, HW)], vr[at, pl.ds(vc, HW)])

                return carry

            @pl.when(needed if compact else needed & unsafe)
            def _():
                lax.fori_loop(0, tiles * tiles, one_pair, 0)

            if not compact:
                pl.when(needed & safe & wide)(lambda: whole(0, row_count, 0))

                @pl.when(needed & safe & jnp.logical_not(wide))
                def _():
                    for w in range(tiles):
                        whole(w * TILE, TILE, w * TILE)

        if has_own:

            @pl.when(jnp.bool_(True) if compact else unsafe)
            def _():
                l_ref[...] = jnp.zeros_like(l_ref)
                a_ref[...] = jnp.zeros_like(a_ref)
                m_ref[...] = jnp.full_like(m_ref, NEG)

            group(jnp.bool_(True), [(k_ref, v_ref, 0, low, low, None)], base=None)

            @pl.when(safe)
            def _():
                fast(0, row_count, text_ref[:, q_cols], text_ref[:, pl.ds(high, HW)], None, valid_ref[...] > 0)

            @pl.when(unsafe)
            def _():
                def one_tile(w, carry):
                    slow(w * TILE, text_ref[:, q_cols], text_ref[:, pl.ds(high, HW)], valid_ref[...] > 0)
                    return carry

                lax.fori_loop(0, tiles, one_tile, 0)
        else:
            ((along_time, along_height, _),) = slabs
            needed = reaches(head, along_time, along_height)

            @pl.when(unsafe | jnp.logical_not(needed))
            def _():
                m_ref[...] = mi_ref[...]
                l_ref[...] = li_ref[...]
                a_ref[...] = ai_ref[...]

        for along_time, along_height, members in slabs:
            needed = reaches(head, along_time, along_height)
            found = []
            for ref_id, row0, dt, dh in members:
                time, height = time_at + dt, height_at + dh
                held = (time >= 0) & (time < lax.axis_size("tm"))
                held = held & (height >= 0) & (height < lax.axis_size("height"))
                ref = slab_refs[ref_id]
                cols = (low, high) if paired else (0, HW)
                found.append((ref, ref, row0) + cols + (held.astype(jnp.int32),))
            group(needed, found, (l_ref, a_ref) if has_own else (li_ref, ai_ref))

        def keep():
            @pl.when(unsafe)
            def _():
                mo_ref[...] = m_ref[...]

            @pl.when(safe)
            def _():
                mo_ref[0:8, :] = jnp.full((8, HW), MARK, jnp.float32)

            lo_ref[...] = l_ref[...]
            ao_ref[...] = a_ref[...]

        def finish(ref, cols):
            total = jnp.sum(l_ref[...], axis=1, keepdims=True)
            ref[:, cols] = (a_ref[...] / total).astype(jnp.bfloat16)

        if ends == "state":
            keep()
        elif ends == "split":
            pl.when(job == 0)(keep)
            pl.when(job != 0)(lambda: finish(oo_ref, pl.ds(0, HW)))
        else:
            finish(out_ref, q_cols)
            if ends == "merge":
                cols = pl.ds(pl.multiple_of((1 - head) * HW, HW), HW)
                out_ref[:, cols] = other_ref[...]
        return carry

    lax.fori_loop(0, jobs, one_head, 0)


SMEM = pl.BlockSpec(memory_space=pltpu.SMEM)
VMEM = pl.BlockSpec(memory_space=pltpu.VMEM)


def attention(jobs, ends, slabs, ext, q, arrays, own=None, state=None, other=None, paired=False):
    rows, feat = q.shape
    scale = math.log2(math.e) / math.sqrt(HW)
    spec = (jobs, own is not None, ends, slabs, len(arrays), paired, scale)
    args = [ext, q] + list(own if own is not None else state) + list(arrays)
    if other is not None:
        args.append(other)
    part = jax.ShapeDtypeStruct((rows, HW), jnp.float32)
    if ends == "state":
        outs = (part,) * 3
    elif ends == "split":
        outs = (part,) * 3 + (jax.ShapeDtypeStruct((rows, HW), jnp.bfloat16),)
    else:
        outs = jax.ShapeDtypeStruct((rows, feat), jnp.bfloat16)
    scores = rows * rows * (sum(len(s[2]) for s in slabs) + 1)
    return pl.pallas_call(
        functools.partial(attention_kernel, spec),
        out_shape=outs,
        in_specs=[SMEM] + [VMEM] * (len(args) - 1),
        out_specs=(VMEM,) * len(outs) if isinstance(outs, tuple) else VMEM,
        scratch_shapes=[pltpu.VMEM((rows, HW), jnp.float32)] * 3,
        compiler_params=pltpu.CompilerParams(vmem_limit_bytes=40 * 1024 * 1024),
        cost_estimate=pl.CostEstimate(
            flops=4 * HW * scores, bytes_accessed=4 * rows * feat * 4, transcendentals=scores
        ),
    )(*args)


def pick_kernel(ext_ref, k_ref, v_ref, h_ref, t_ref):
    for out_ref, axis in ((h_ref, 1), (t_ref, 0)):
        cols = pl.ds(pl.multiple_of((1 - ext_ref[0, axis]) * HW, HW), HW)
        out_ref[:, :HW] = k_ref[:, cols]
        out_ref[:, HW:] = v_ref[:, cols]


def pick(ext, k, v):
    rows = k.shape[0]
    part = jax.ShapeDtypeStruct((rows, 2 * HW), k.dtype)
    return pl.pallas_call(
        pick_kernel,
        in_specs=[SMEM, VMEM, VMEM],
        out_specs=(VMEM, VMEM),
        out_shape=(part, part),
        cost_estimate=pl.CostEstimate(flops=0, bytes_accessed=16 * rows * HW, transcendentals=0),
        name="pick",
    )(ext, k, v)


def shards(video_q, video_k, video_v, text_k, text_v, text_valid, extent):
    rows, feat = video_q.shape[2:]
    q, k, v = (a.reshape(rows, feat) for a in (video_q, video_k, video_v))
    hn = lax.axis_size("height")
    t_rings, h_rings = rings("tm"), rings("height")
    valid = text_valid.reshape(1, -1)

    table = 0
    for c in range(16):
        t0, h0, t1, h1 = (c >> i & 1 for i in range(4))
        crowded = (t0 and t1) or (h0 and h1)
        table |= (2 if crowded else int((t0 and h0) or (t1 and h1))) << (2 * c)
    table -= (table >> 31) << 32
    shift = jnp.sum(extent * jnp.array([[2, 4, 0], [8, 16, 0]], jnp.int32))
    branch = lax.shift_right_arithmetic(jnp.int32(table), shift) & 3

    def text_tokens(text_k, text_v):
        mine = jnp.concatenate([text_k, text_v], axis=1)
        copies = jnp.broadcast_to(mine[None], (hn,) + mine.shape)
        got = lax.all_to_all(copies, "height", 0, 0)
        return got.reshape(-1, mine.shape[1])

    def exchange(x, axis, pairs):
        up, down = pairs
        before = lax.ppermute(x, axis, up)
        after = lax.ppermute(x, axis, down)
        return before, after

    def sparse(diagonal):
        def run(q, k, v, text_k, text_v, valid, ext):
            kv_h, kv_t = pick(ext, k, v)
            h0, h1 = exchange(kv_h, "height", h_rings)
            t0, t1 = exchange(kv_t, "tm", t_rings)
            text = text_tokens(text_k, text_v)
            m, l, a, other = attention(
                2, "split", ((True, False, ((0, 0, -1, 0), (1, 0, 1, 0))),),
                ext, q, (t0, t1), own=(k, v, text, valid),
            )
            hs = ((False, True, ((0, 0, 0, -1), (1, 0, 0, 1))),)
            if not diagonal:
                return attention(1, "merge", hs, ext, q, (h0, h1), state=(m, l, a), other=other)
            d0, d1 = exchange(jnp.concatenate([h0, h1], axis=0), "tm", t_rings)
            m, l, a = attention(1, "state", hs, ext, q, (h0, h1), state=(m, l, a))
            corners = ((0, 0, -1, -1), (0, rows, -1, 1), (1, 0, 1, -1), (1, rows, 1, 1))
            ds = ((True, True, corners),)
            return attention(
                1, "merge", ds, ext, q, (d0, d1),
                state=(m, l, a), other=other,
            )

        return run

    def dense(q, k, v, text_k, text_v, valid, ext):
        kv = jnp.concatenate([k, v], axis=1)
        h0, h1 = exchange(kv, "height", h_rings)
        text = text_tokens(text_k, text_v)
        three = jnp.concatenate([h0, kv, h1], axis=0)
        t0, t1 = exchange(three, "tm", t_rings)
        slabs = (
            (False, True, ((0, 0, 0, -1), (1, 0, 0, 1))),
            (True, False, ((2, rows, -1, 0), (3, rows, 1, 0))),
            (True, True, ((2, 0, -1, -1), (2, 2 * rows, -1, 1))),
            (True, True, ((3, 0, 1, -1), (3, 2 * rows, 1, 1))),
        )
        return attention(
            2, "all", slabs, ext, q, (h0, h1, t0, t1),
            own=(k, v, text, valid), paired=True,
        )

    out = lax.switch(
        branch, [sparse(False), sparse(True), dense], q, k, v, text_k, text_v, valid, extent
    )
    return out.reshape(video_q.shape)


def solution(mesh):
    video = P("tm", "height", None, None)
    return jax.shard_map(
        shards,
        mesh=mesh,
        in_specs=(video, video, video, P("height", None), P("height", None), P(), P()),
        out_specs=video,
        check_vma=False,
    )
```

time: 81.2 us -> 114 us (1.40)
  the two profiles are of different devices: /device:TPU:38 before, /device:TPU:15 now
where the time goes in v2:
time: 114 us; the launch traced here: 113 us
  Pallas kernels  44.8 us (39%)
  starting transfers between devices  36.3 us (32%)
  waiting for transfers between devices  27 us (24%)
  local copies, waits for them, and re-layouts  2.31 us (2%)
  other arithmetic  1.34 us (1%)
    pallas_call x3, Pallas kernels, attention(): pl.pallas_call(functools.partial(attention_kernel, spec), out_shape=outs,...  42.6 us
    ppermute x3, waiting for transfers between devices, exchange(): before = lax.ppermute(x, axis, up)  18 us
    ppermute x3, starting transfers between devices, exchange(): before = lax.ppermute(x, axis, up)  14 us
    ppermute x3, starting transfers between devices, exchange(): after = lax.ppermute(x, axis, down)  12.3 us
    all_to_all x1, starting transfers between devices, text_tokens(): got = lax.all_to_all(copies, 'height', 0, 0)  9.96 us
    ppermute x3, waiting for transfers between devices, exchange(): after = lax.ppermute(x, axis, down)  9 us
  transfers between devices with their start and end apart: 7, of which 4 were waited for; matrix products, arithmetic and copies ran while one was open for 1% of the time, Pallas kernels for 26%

profile of v2, /device:TPU:15, one launch (start us, length us, event | category | flops | bytes accessed | tf_op | source)
XLA Modules:
  0.0 113.3 jit_solution(16709093276376043627)
XLA Ops:
  0.0 1.3 %multiply_reduce_fusion = s32[]{:T(128)} fusion(s32[2,3]{1,0:T(2,128)} %param.17, s32[2,3]{1,0:T(2,128)} %constant.10.clone), kind=kLoop, calls=%fused_computation.8 | loop fusion | flops 11 | bytes 52 | tf_op jit(solution)/shard_map/reduce_sum | solution.py:303
  2.0 111.1 %conditional.1 = (bf16[1,1,768,256]{3,2,1,0:T(8,128)(2,1)}) conditional(s32[]{:T(128)} %clamp.3, (bf16[8,256]{1,0:T(8,128)(2,1)}, bf16[8,256]{1,0:T(8,128)(2,1)}, s32[2,3]{1,0:T(2,128)}, bf16[768,256]{1,0:T(8,128)(2,1)}, bf16[768,256]{1,0:T(8,128)(2,1)}, /*index=5*/bf16[768,256]{1,0:T(8,128)(2,1)}, s32[1,256]{1,0:T(1,128)}) %tuple.34, ...), branch_computations={%region_1.0_spmd, %region_2.0_spmd, %region_3.0_spmd} | conditional | flops 3321905152 | bytes 40169932 | solution.py:359
  2.0 0.0 copy-start.2
  2.0 0.0 copy-start.4
  2.0 0.0 copy-start.7
  2.0 0.0 copy-start.12
  2.1 2.2 %pick.3 = (bf16[768,256]{1,0:T(8,128)(2,1)}, bf16[768,256]{1,0:T(8,128)(2,1)}) custom-call(s32[2,3]{1,0:T(2,128)} %get-tuple-element.65.ext_ref.refs_0_, bf16[768,256]{1,0:T(8,128)(2,1)} %get-tuple-element.67.k_ref.refs_2_, bf16[768,256]{1,0:T(8,128)(2,1)} %get-tuple-element.68.v_ref.refs_3_), custom_call_target="tpu_custom_call" | custom-call | bytes 1572864 | tf_op jit(solution)/shard_map/cond/branch_1_fun/pick/pallas_call | solution.py:280
  4.2 5.8 %collective-permute-start.6 = (bf16[768,256]{1,0:T(8,128)(2,1)}, bf16[768,256]{1,0:T(8,128)(2,1)S(1)}, u32[]{:S(2)}, u32[]{:S(2)}) collective-permute-start(bf16[768,256]{1,0:T(8,128)(2,1)} %get-tuple-element.76), channel_id=1, source_target_pairs={{0,1},{1,2},{2,3},{3,4},{4,5},{5,6},{6,7},{7,8},{8,9},{9,10},{10,1... | collective-permute-start | bytes 1179656 | tf_op jit(solution)/shard_map/cond/branch_1_fun/ppermute | solution.py:314
  10.0 6.7 %collective-permute-start.7 = (bf16[768,256]{1,0:T(8,128)(2,1)}, bf16[768,256]{1,0:T(8,128)(2,1)S(1)}, u32[]{:S(2)}, u32[]{:S(2)}) collective-permute-start(bf16[768,256]{1,0:T(8,128)(2,1)} %get-tuple-element.76), channel_id=1, source_target_pairs={{1,0},{2,1},{3,2},{4,3},{5,4},{6,5},{7,6},{8,7},{9,8},{10,9},{11,1... | collective-permute-start | bytes 1179656 | tf_op jit(solution)/shard_map/cond/branch_1_fun/ppermute | solution.py:315
  16.7 13.1 %collective-permute-done.6.refs_5_ = bf16[768,256]{1,0:T(8,128)(2,1)S(1)} collective-permute-done((bf16[768,256]{1,0:T(8,128)(2,1)}, bf16[768,256]{1,0:T(8,128)(2,1)S(1)}, u32[]{:S(2)}, u32[]{:S(2)}) %collective-permute-start.6) | collective-permute-done | bytes 393248 | tf_op jit(solution)/shard_map/cond/branch_1_fun/ppermute | solution.py:314
  29.8 0.8 constant_dynamic-update-slice_fusion.1
  30.5 4.6 %collective-permute-done.7.refs_6_ = bf16[768,256]{1,0:T(8,128)(2,1)S(1)} collective-permute-done((bf16[768,256]{1,0:T(8,128)(2,1)}, bf16[768,256]{1,0:T(8,128)(2,1)S(1)}, u32[]{:S(2)}, u32[]{:S(2)}) %collective-permute-start.7) | collective-permute-done | bytes 393248 | tf_op jit(solution)/shard_map/cond/branch_1_fun/ppermute | solution.py:315
  35.2 0.8 constant_dynamic-update-slice_fusion
  36.0 2.0 %collective-permute-start.8 = (bf16[1536,256]{1,0:T(8,128)(2,1)}, bf16[1536,256]{1,0:T(8,128)(2,1)S(1)}, u32[]{:S(2)}, u32[]{:S(2)}) collective-permute-start(bf16[1536,256]{1,0:T(8,128)(2,1)} %constant_dynamic-update-slice_fusion), channel_id=1, source_target_pairs={{0,32},{32,64},{64,96},{96,128},{128,160},{160,192},{192,224},{224... | collective-permute-start | bytes 2359304 | tf_op jit(solution)/shard_map/cond/branch_1_fun/ppermute | solution.py:314
  38.0 3.5 %collective-permute-start.9 = (bf16[1536,256]{1,0:T(8,128)(2,1)}, bf16[1536,256]{1,0:T(8,128)(2,1)S(1)}, u32[]{:S(2)}, u32[]{:S(2)}) collective-permute-start(bf16[1536,256]{1,0:T(8,128)(2,1)} %constant_dynamic-update-slice_fusion), channel_id=1, source_target_pairs={{32,0},{64,32},{96,64},{128,96},{160,128},{192,160},{224,192},{256... | collective-permute-start | bytes 2359304 | tf_op jit(solution)/shard_map/cond/branch_1_fun/ppermute | solution.py:315
  41.5 0.0 copy-done.2
  41.5 0.0 copy-done.4
  41.5 0.7 broadcast_in_dim.8
  42.2 10.0 %all-to-all-start.1 = ((bf16[32,8,512]{2,1,0:T(8,128)(2,1)}), bf16[32,8,512]{2,1,0:T(8,128)(2,1)S(1)}, u32[]{:S(2)}, u32[]{:S(2)}) async-start(bf16[32,8,512]{2,1,0:T(8,128)(2,1)} %broadcast_in_dim.8), calls=%async_computation.1 | async-start | bytes 524288 | tf_op jit(solution)/shard_map/cond/branch_1_fun/all_to_all | solution.py:309
  52.2 6.2 %collective-permute-start.4 = (bf16[768,256]{1,0:T(8,128)(2,1)}, bf16[768,256]{1,0:T(8,128)(2,1)S(1)}, u32[]{:S(2)}, u32[]{:S(2)}) collective-permute-start(bf16[768,256]{1,0:T(8,128)(2,1)} %get-tuple-element.72), channel_id=1, source_target_pairs={{0,32},{32,64},{64,96},{96,128},{128,160},{160,192},{192,224},{224... | collective-permute-start | bytes 1179656 | tf_op jit(solution)/shard_map/cond/branch_1_fun/ppermute | solution.py:314
  58.4 2.2 %collective-permute-start.5 = (bf16[768,256]{1,0:T(8,128)(2,1)}, bf16[768,256]{1,0:T(8,128)(2,1)S(1)}, u32[]{:S(2)}, u32[]{:S(2)}) collective-permute-start(bf16[768,256]{1,0:T(8,128)(2,1)} %get-tuple-element.72), channel_id=1, source_target_pairs={{32,0},{64,32},{96,64},{128,96},{160,128},{192,160},{224,192},{256... | collective-permute-start | bytes 1179656 | tf_op jit(solution)/shard_map/cond/branch_1_fun/ppermute | solution.py:315
  60.6 5.0 %collective-permute-done.4.refs_6_ = bf16[768,256]{1,0:T(8,128)(2,1)S(1)} collective-permute-done((bf16[768,256]{1,0:T(8,128)(2,1)}, bf16[768,256]{1,0:T(8,128)(2,1)S(1)}, u32[]{:S(2)}, u32[]{:S(2)}) %collective-permute-start.4) | collective-permute-done | bytes 393248 | tf_op jit(solution)/shard_map/cond/branch_1_fun/ppermute | solution.py:314
  65.6 4.4 %collective-permute-done.5.refs_7_ = bf16[768,256]{1,0:T(8,128)(2,1)S(1)} collective-permute-done((bf16[768,256]{1,0:T(8,128)(2,1)}, bf16[768,256]{1,0:T(8,128)(2,1)S(1)}, u32[]{:S(2)}, u32[]{:S(2)}) %collective-permute-start.5) | collective-permute-done | bytes 393248 | tf_op jit(solution)/shard_map/cond/branch_1_fun/ppermute | solution.py:315
  69.9 0.0 all-to-all-done.1
  69.9 0.0 copy-start.10
  69.9 0.0 copy-done.7
  69.9 0.0 copy-done.12
  69.9 22.5 %branch_1_fun.3 = (f32[768,128]{1,0:T(8,128)S(1)}, f32[768,128]{1,0:T(8,128)S(1)}, f32[768,128]{1,0:T(8,128)S(1)}, bf16[768,128]{1,0:T(8,128)(2,1)S(1)}) custom-call(s32[2,3]{1,0:T(2,128)S(1)} %copy-done.7, bf16[768,256]{1,0:T(8,128)(2,1)} %get-tuple-element.66.refs_1_, bf16[768,256]{1,0:T(8,128)(2,1)} %get-tuple-element.67.k_ref.refs_2_, ...), custom_call_target="tpu_custom_call" | custom-call | flops 905969664 | bytes 3145728 | tf_op jit(solution)/shard_map/cond/branch_1_fun/pallas_call | solution.py:257
  92.5 0.0 copy-done.10
  92.5 6.7 %branch_1_fun.4 = (f32[768,128]{1,0:T(8,128)S(1)}, f32[768,128]{1,0:T(8,128)S(1)}, f32[768,128]{1,0:T(8,128)S(1)}) custom-call(s32[2,3]{1,0:T(2,128)S(1)} %copy-done.7, bf16[768,256]{1,0:T(8,128)(2,1)S(1)} %copy-done.10, f32[768,128]{1,0:T(8,128)S(1)} %get-tuple-element.73.refs_2_, f32[768,128]{1,0:T(8,128)S(1)} %get-tuple-element.74.refs_3_, ...), custom_call_target="tpu_custom_call" | custom-call | flops 905969664 | bytes 3145728 | tf_op jit(solution)/shard_map/cond/branch_1_fun/pallas_call | solution.py:257
  99.2 0.0 collective-permute-done.8.refs_5_
  99.2 0.0 collective-permute-done.9.refs_6_
  99.2 13.4 %branch_1_fun.5 = bf16[768,256]{1,0:T(8,128)(2,1)} custom-call(s32[2,3]{1,0:T(2,128)S(1)} %copy-done.7, bf16[768,256]{1,0:T(8,128)(2,1)S(1)} %copy-done.10, f32[768,128]{1,0:T(8,128)S(1)} %get-tuple-element.77.refs_2_, f32[768,128]{1,0:T(8,128)S(1)} %get-tuple-element.78.refs_3_, f32[768,128]{1,0:T(8,128)S(1)} %get-tuple-element.79.refs_4_, ...), custom_call_target="tpu_custom_call" | custom-call | flops 1509949440 | bytes 3145728 | tf_op jit(solution)/shard_map/cond/branch_1_fun/pallas_call | solution.py:257
  (1 shorter events, 0.0 us)
Async XLA Ops:
  2.0 39.5 %copy-start.2 = (bf16[8,256]{1,0:T(8,128)(2,1)S(1)}, bf16[8,256]{1,0:T(8,128)(2,1)}, u32[]{:S(2)}) copy-start(bf16[8,256]{1,0:T(8,128)(2,1)} %get-tuple-element.69) | copy-start | bytes 12292 | tf_op jit(solution)/shard_map/cond
  2.0 39.5 %copy-start.4 = (bf16[8,256]{1,0:T(8,128)(2,1)S(1)}, bf16[8,256]{1,0:T(8,128)(2,1)}, u32[]{:S(2)}) copy-start(bf16[8,256]{1,0:T(8,128)(2,1)} %get-tuple-element.70) | copy-start | bytes 12292 | tf_op jit(solution)/shard_map/cond
  2.0 67.9 %copy-start.7 = (s32[2,3]{1,0:T(2,128)S(1)}, s32[2,3]{1,0:T(2,128)}, u32[]{:S(2)}) copy-start(s32[2,3]{1,0:T(2,128)} %get-tuple-element.65.ext_ref.refs_0_) | copy-start | bytes 76 | tf_op jit(solution)/shard_map/cond
  2.0 67.9 %copy-start.12 = (s32[1,256]{1,0:T(1,128)S(1)}, s32[1,256]{1,0:T(1,128)}, u32[]{:S(2)}) copy-start(s32[1,256]{1,0:T(1,128)} %get-tuple-element.71.refs_5_) | copy-start | bytes 3076 | tf_op jit(solution)/shard_map/cond
  4.2 25.5 %collective-permute-start.6 = (bf16[768,256]{1,0:T(8,128)(2,1)}, bf16[768,256]{1,0:T(8,128)(2,1)S(1)}, u32[]{:S(2)}, u32[]{:S(2)}) collective-permute-start(bf16[768,256]{1,0:T(8,128)(2,1)} %get-tuple-element.76), channel_id=1, source_target_pairs={{0,1},{1,2},{2,3},{3,4},{4,5},{5,6},{6,7},{7,8},{8,9},{9,10},{10,1... | collective-permute-start | bytes 1179656 | tf_op jit(solution)/shard_map/cond/branch_1_fun/ppermute | solution.py:314
  10.0 25.1 %collective-permute-start.7 = (bf16[768,256]{1,0:T(8,128)(2,1)}, bf16[768,256]{1,0:T(8,128)(2,1)S(1)}, u32[]{:S(2)}, u32[]{:S(2)}) collective-permute-start(bf16[768,256]{1,0:T(8,128)(2,1)} %get-tuple-element.76), channel_id=1, source_target_pairs={{1,0},{2,1},{3,2},{4,3},{5,4},{6,5},{7,6},{8,7},{9,8},{10,9},{11,1... | collective-permute-start | bytes 1179656 | tf_op jit(solution)/shard_map/cond/branch_1_fun/ppermute | solution.py:315
  36.0 63.2 %collective-permute-start.8 = (bf16[1536,256]{1,0:T(8,128)(2,1)}, bf16[1536,256]{1,0:T(8,128)(2,1)S(1)}, u32[]{:S(2)}, u32[]{:S(2)}) collective-permute-start(bf16[1536,256]{1,0:T(8,128)(2,1)} %constant_dynamic-update-slice_fusion), channel_id=1, source_target_pairs={{0,32},{32,64},{64,96},{96,128},{128,160},{160,192},{192,224},{224... | collective-permute-start | bytes 2359304 | tf_op jit(solution)/shard_map/cond/branch_1_fun/ppermute | solution.py:314
  38.0 61.2 %collective-permute-start.9 = (bf16[1536,256]{1,0:T(8,128)(2,1)}, bf16[1536,256]{1,0:T(8,128)(2,1)S(1)}, u32[]{:S(2)}, u32[]{:S(2)}) collective-permute-start(bf16[1536,256]{1,0:T(8,128)(2,1)} %constant_dynamic-update-slice_fusion), channel_id=1, source_target_pairs={{32,0},{64,32},{96,64},{128,96},{160,128},{192,160},{224,192},{256... | collective-permute-start | bytes 2359304 | tf_op jit(solution)/shard_map/cond/branch_1_fun/ppermute | solution.py:315
  42.2 27.7 %all-to-all-start.1 = ((bf16[32,8,512]{2,1,0:T(8,128)(2,1)}), bf16[32,8,512]{2,1,0:T(8,128)(2,1)S(1)}, u32[]{:S(2)}, u32[]{:S(2)}) async-start(bf16[32,8,512]{2,1,0:T(8,128)(2,1)} %broadcast_in_dim.8), calls=%async_computation.1 | async-start | bytes 524288 | tf_op jit(solution)/shard_map/cond/branch_1_fun/all_to_all | solution.py:309
  52.2 13.4 %collective-permute-start.4 = (bf16[768,256]{1,0:T(8,128)(2,1)}, bf16[768,256]{1,0:T(8,128)(2,1)S(1)}, u32[]{:S(2)}, u32[]{:S(2)}) collective-permute-start(bf16[768,256]{1,0:T(8,128)(2,1)} %get-tuple-element.72), channel_id=1, source_target_pairs={{0,32},{32,64},{64,96},{96,128},{128,160},{160,192},{192,224},{224... | collective-permute-start | bytes 1179656 | tf_op jit(solution)/shard_map/cond/branch_1_fun/ppermute | solution.py:314
  58.4 11.5 %collective-permute-start.5 = (bf16[768,256]{1,0:T(8,128)(2,1)}, bf16[768,256]{1,0:T(8,128)(2,1)S(1)}, u32[]{:S(2)}, u32[]{:S(2)}) collective-permute-start(bf16[768,256]{1,0:T(8,128)(2,1)} %get-tuple-element.72), channel_id=1, source_target_pairs={{32,0},{64,32},{96,64},{128,96},{160,128},{192,160},{224,192},{256... | collective-permute-start | bytes 1179656 | tf_op jit(solution)/shard_map/cond/branch_1_fun/ppermute | solution.py:315
  69.9 22.6 %copy-start.10 = (bf16[768,256]{1,0:T(8,128)(2,1)S(1)}, bf16[768,256]{1,0:T(8,128)(2,1)}, u32[]{:S(2)}) copy-start(bf16[768,256]{1,0:T(8,128)(2,1)} %get-tuple-element.66.refs_1_) | copy-start | bytes 1179652 | tf_op jit(solution)/shard_map/cond
